TPU v7x, 256 devices: a whole 4x4x8 slice. The times are simulated.
256 devices in a mesh: row: 8 (over y, z_hi), col: 4 (over x), layer: 8 (over z_lo, core).
Axes of the slice: x: 4, y: 4, z: 8 (z_hi: 2, z_lo: 4; z = z_hi * 4 + z_lo), core: 2. Of those that a mesh axis runs over, the one named last changes fastest.
Arguments:
- coeffs: float32 [4096, 4096], P(('row', 'col'), 'layer'), may hold values from -6 to 6
- hblocks: float32 [256, 128, 128], P('layer'), may hold values from -0.1875 to 0.1875
- hcount: int32 [32], replicated, may hold values from 1 to 16, 256 in all
- hcols: int32 [256], P('layer'), may hold values from 0 to 31
Outputs:
- sigma: float32 [4096, 4096], P(('row', 'col'), 'layer')
Inputs may be any that keep to these rules, and one draw needn't show every extreme that they name: `hcount`: the blocks of a row stand together in hcols and hblocks, rows in order; the counts sum to 256 and some row holds 16. `hcols`: a row may name a column more than once; such blocks add.
All inputs are finite; a program needn't handle non-finite values.
Results may differ from a plain program's by a relative error of at most 0.00007.
Values sent between devices are 32-bit elements; how exact they have to be, the bound alone decides.
No kernel may reach another device: no remote copies, remote signals or barrier semaphores. Data moves between devices by JAX's collectives and lax.ppermute only.
A program may use at most 64 MiB of HBM per device.

v0:
```python
import jax
import jax.numpy as jnp
from jax import lax
from jax.experimental import pallas as pl
from jax.experimental.pallas import tpu as pltpu
from jax.sharding import Mesh
from jax.sharding import PartitionSpec as P

ROWS = ("y", "h", "x")
ANY = pl.BlockSpec(memory_space=pl.ANY)
VMEM = pl.BlockSpec(memory_space=pltpu.VMEM)
SMEM = pl.BlockSpec(memory_space=pltpu.SMEM)
F32 = jnp.float32
BF16 = jnp.bfloat16
CONTRACT = (((1,), (1,)), ((), ()))
OFFSETS = (0, -1, 1, 2)


def params(mib):
    return pltpu.CompilerParams(vmem_limit_bytes=mib << 20)


def cost(flops, moved):
    return pl.CostEstimate(flops=flops, bytes_accessed=moved, transcendentals=0)


def shape(*dims, kind=F32):
    return jax.ShapeDtypeStruct(dims, kind)


def turn_kernel(c_ref, after, at_ref):
    for t in range(4):
        turned = jnp.transpose(c_ref[:, 128 * t : 128 * (t + 1)]).reshape(8, 16, 128)
        at_ref[8 * t : 8 * (t + 1), 0] = turned
        at_ref[8 * t : 8 * (t + 1), 1] = turned


def join_kernel(where, cols, own, down, up, far, out_ref):
    x = where[1]
    for by, part in zip(OFFSETS, (own, down, up, far)):
        out_ref[pl.ds(2 * jnp.bitwise_and(x + by + 4, 3), 2)] = part[...]


def halves(value):
    high = value.astype(BF16)
    return high, (value - high.astype(F32)).astype(BF16)


def product(left, block):
    high, low = halves(block)
    rows = left.shape[0] // 2
    one = lax.dot_general(left, high, CONTRACT, preferred_element_type=F32)
    two = lax.dot_general(left[:rows], low, CONTRACT, preferred_element_type=F32)
    return one[:rows] + (one[rows:] + two)


def alpha_pass(first, count, hbuf, cols, owners, table, stack, acc):
    @pl.loop(0, count // 4)
    def _(step):
        at = first + 4 * step
        terms = []
        for u in range(4):
            spot = table + at + u
            terms.append((owners[spot], product(stack[cols[spot]], hbuf[at + u])))
        for owner, term in terms:
            acc[owner] += term


def beta_pass(table, hbuf, cols, slots, stack, acc, list_ref):
    def note(n, count):
        list_ref[count] = n
        return count + jnp.where(slots[table + n] < 16, 1, 0)

    count = lax.fori_loop(0, 64, note, 0)
    list_ref[count] = 0

    @pl.loop(0, lax.shift_right_logical(count + 1, 1))
    def _(step):
        terms = []
        for u in range(2):
            n = list_ref[2 * step + u]
            column = cols[table + n]
            left = stack[4 * lax.shift_right_logical(column, 3) + jnp.bitwise_and(column, 3)]
            slot = jnp.where(2 * step + u < count, slots[table + n], 16)
            terms.append((slot, product(left, hbuf[n])))
        for slot, term in terms:
            acc[slot] += term


def beta_near_kernel(
    where, cols, slots, w0, w1, w2, w3, h0, h1, out_b, stack_b,
    wide, hbuf, acc, list_ref, sem_w, sem_h,
):
    z = where[2]
    loads = [
        pltpu.make_async_copy(w, wide.at[k], sem_w.at[k]) for k, w in enumerate((w0, w1, w2, w3))
    ]
    for load in loads:
        load.start()
    chunks = [
        pltpu.make_async_copy(h, hbuf.at[pl.ds(32 * n, 32)], sem_h.at[n])
        for n, h in enumerate((h0, h1))
    ]
    for chunk in chunks:
        chunk.start()
    acc[...] = jnp.zeros_like(acc)
    for k, load in enumerate(loads):
        home = 4 * jnp.bitwise_and(z - k + 4, 3)
        load.wait()
        for t in range(4):
            high, low = halves(wide[k, :, 128 * t : 128 * (t + 1)])
            stack_b[home + t, :128] = high
            stack_b[home + t, 128:] = low
    for chunk in chunks:
        chunk.wait()
    beta_pass(0, hbuf, cols, slots, stack_b, acc, list_ref)
    out_b[...] = acc[:16]


def alpha_near_kernel(cols, owners, a_ref, h0, h1, acc_a, stack_a, hbuf, sem_h):
    chunks = []
    for n in range(4):
        source = (h0, h1)[n // 2].at[pl.ds(16 * (n % 2), 16)]
        chunks.append(pltpu.make_async_copy(source, hbuf.at[pl.ds(16 * n, 16)], sem_h.at[n]))
    for chunk in chunks:
        chunk.start()
    acc_a[...] = jnp.zeros_like(acc_a)

    @pl.loop(0, 32)
    def _(j):
        high, low = halves(a_ref[j])
        stack_a[j, :32] = high
        stack_a[j, 32:] = low

    for n, chunk in enumerate(chunks):
        chunk.wait()
        alpha_pass(16 * n, 16, hbuf, cols, owners, 0, stack_a, acc_a)


FAR = ((0, 0, 8), (-1, 0, 8), (1, 0, 8), (2, 0, 4), (2, 4, 4))


def far_kernel(where, cols, owners, slots, in_a, in_stack_a, in_b, in_stack_b, *refs):
    sources, (out_a, keep_b, send_b) = refs[:10], refs[10:13]
    acc_b, stack_a, stack_b, hbuf, list_ref, sem_a, sem_h = refs[13:]
    y, core = where[0], where[3]
    loads = [
        pltpu.make_async_copy(in_a, out_a, sem_a.at[0]),
        pltpu.make_async_copy(in_stack_a, stack_a, sem_a.at[1]),
        pltpu.make_async_copy(in_b, acc_b.at[pl.ds(0, 16)], sem_a.at[2]),
        pltpu.make_async_copy(in_stack_b, stack_b, sem_a.at[3]),
    ]
    chunks = []
    for side in range(2):
        for n, (by, extra, size) in enumerate(FAR):
            home = 32 * side + 8 * jnp.bitwise_and(y + by + 4, 3) + extra
            copy = pltpu.make_async_copy(
                sources[5 * side + n], hbuf.at[pl.ds(home, size)], sem_h.at[5 * side + n]
            )
            chunks.append((copy, home, size))
    for load in loads[:2]:
        load.start()
    for chunk, *_ in chunks:
        chunk.start()
    for load in loads[2:]:
        load.start()
    for load in loads[:2]:
        load.wait()
    for chunk, home, size in chunks:
        chunk.wait()
        alpha_pass(home, size, hbuf, cols, owners, 64, stack_a, out_a)
    for load in loads[2:]:
        load.wait()
    beta_pass(64, hbuf, cols, slots, stack_b, acc_b, list_ref)
    for plane in range(2):
        keep_b[4 * plane : 4 * plane + 4] = acc_b[pl.ds(8 * plane + 4 * core, 4)]
        send_b[4 * plane : 4 * plane + 4] = acc_b[pl.ds(8 * plane + 4 * (1 - core), 4)]


def cores_kernel(keep_ref, got_ref, own_ref, other_ref):
    own_ref[...] = keep_ref[:4] + got_ref[:4]
    other_ref[...] = keep_ref[4:] + got_ref[4:]


def final_kernel(back_ref, own_ref, got_ref, out_ref):
    for t in range(4):
        span = slice(128 * t, 128 * (t + 1))
        total = back_ref[8 * t : 8 * (t + 1), 0] + back_ref[8 * t : 8 * (t + 1), 1]
        out_ref[:, span] = jnp.transpose(total.reshape(128, 128)) + (own_ref[t] + got_ref[t])


def shift(value, axis, by):
    return lax.ppermute(value, axis, [(i, (i + by) % 4) for i in range(4)])


def swap(value):
    return lax.ppermute(value, "c", [(0, 1), (1, 0)])


def pair(value):
    return lax.ppermute(value, "z", [(0, 1), (1, 0), (2, 3), (3, 2)])


def ring(value, axis):
    half = value.shape[0] // 2
    down, up = shift(value, axis, 1), shift(value, axis, -1)
    return value, down, up, shift(down[:half], axis, 1), shift(up[half:], axis, -1)


def tables(hcount, hcols, z, c):
    near_cols = jnp.concatenate([hcols, swap(hcols)])
    cols = jnp.concatenate([near_cols, pair(near_cols)])
    marks = jnp.arange(32, dtype=jnp.int32)
    row_end = jnp.sum(jnp.where(marks[:, None] <= marks[None, :], hcount[:, None], 0), axis=0)
    shard = jnp.stack([2 * z + c, 2 * z + 1 - c, 2 * (z ^ 1) + c, 2 * (z ^ 1) + 1 - c])
    index = (32 * shard[:, None].astype(jnp.int32) + marks[None, :]).reshape(128)
    owners = jnp.sum((row_end[None, :] <= index[:, None]).astype(jnp.int32), axis=1)
    inner = (z == 1) | (z == 2)
    slots = jnp.where(owners // 8 == z, owners % 8, 16)
    slots = jnp.where(inner & (owners // 8 == 3 - z), 8 + owners % 8, slots)
    return cols, owners, jnp.where((cols // 4) % 2 == c, slots, 16)


def call(kernel, outs, in_specs, *args, scratch=(), mib=16, work=(0, 1 << 20)):
    single = not isinstance(outs, tuple)
    return pl.pallas_call(
        kernel,
        out_shape=outs,
        in_specs=in_specs,
        out_specs=VMEM if single else (VMEM,) * len(outs),
        scratch_shapes=scratch,
        compiler_params=params(mib),
        cost_estimate=cost(*work),
        name=kernel.__name__,
    )(*args)


def local(coeffs, hblocks, hcount, hcols):
    y, x, z, c = (lax.axis_index(n) for n in ("y", "x", "z", "c"))
    where = jnp.stack([y, x, z, c]).astype(jnp.int32)
    cols, owners, slots = tables(hcount, hcols, z, c)

    near_swapped = swap(hblocks)
    piece = pair(lax.dynamic_slice_in_dim(hblocks, 2 * (4 * y + x), 2, axis=0))
    at = call(turn_kernel, shape(32, 2, 16, 128), [VMEM, ANY], coeffs, piece)
    moved = lax.all_to_all(at.reshape(1024, 128), ROWS + ("z",), 0, 0, tiled=True)
    rows = [coeffs] + [shift(coeffs, "z", k) for k in (1, 2, 3)]
    joined = call(
        join_kernel, shape(8, 128, 128), [SMEM] * 2 + [VMEM] * 4,
        where, cols, piece, *(shift(piece, "x", by) for by in (1, -1, 2)),
    )
    far = ring(joined, "y")
    far_swapped = [swap(part) for part in far]

    out_b, stack_b = call(
        beta_near_kernel,
        (shape(16, 128, 128), shape(16, 256, 128, kind=BF16)),
        [SMEM] * 3 + [ANY] * 6,
        where, cols, slots, *rows, hblocks, near_swapped,
        scratch=[
            pltpu.VMEM((4, 128, 512), F32),
            pltpu.VMEM((64, 128, 128), F32),
            pltpu.VMEM((17, 128, 128), F32),
            pltpu.SMEM((72,), jnp.int32),
            pltpu.SemaphoreType.DMA((4,)),
            pltpu.SemaphoreType.DMA((2,)),
        ],
        mib=24,
        work=(6 * 32 * 128 * 128 * 128, 7 << 20),
    )
    acc_a, stack_a = call(
        alpha_near_kernel,
        (shape(32, 32, 128), shape(32, 64, 128, kind=BF16)),
        [SMEM] * 2 + [VMEM] + [ANY] * 2,
        cols, owners, moved.reshape(32, 32, 128), hblocks, near_swapped,
        scratch=[pltpu.VMEM((64, 128, 128), F32), pltpu.SemaphoreType.DMA((4,))],
        mib=24,
        work=(6 * 64 * 64 * 128 * 128, 7 << 20),
    )
    out_a, keep_b, send_b = call(
        far_kernel,
        (shape(32, 32, 128), shape(8, 128, 128), shape(8, 128, 128)),
        [SMEM] * 4 + [ANY] * 14,
        where, cols, owners, slots, acc_a, stack_a, out_b, stack_b, *far, *far_swapped,
        scratch=[
            pltpu.VMEM((17, 128, 128), F32),
            pltpu.VMEM((32, 64, 128), BF16),
            pltpu.VMEM((16, 256, 128), BF16),
            pltpu.VMEM((64, 128, 128), F32),
            pltpu.SMEM((72,), jnp.int32),
            pltpu.SemaphoreType.DMA((4,)),
            pltpu.SemaphoreType.DMA((10,)),
        ],
        mib=24,
        work=(6 * 64 * 64 * 128 * 128, 8 << 20),
    )

    back = lax.all_to_all(out_a.reshape(1024, 128), ROWS + ("z",), 0, 0, tiled=True)
    own, other = call(cores_kernel, (shape(4, 128, 128),) * 2, [VMEM] * 2, keep_b, swap(send_b))
    got = lax.ppermute(other, "z", [(1, 2), (2, 1)])
    return call(
        final_kernel, shape(128, 512), [VMEM] * 3, back.reshape(32, 2, 16, 128), own, got
    )


def solution(mesh):
    fine = Mesh(mesh.devices.reshape(4, 2, 4, 4, 2), ("y", "h", "x", "z", "c"))
    in_specs = (P(ROWS, ("z", "c")), P(("z", "c"), None, None), P(), P(("z", "c")))
    out_specs = P(ROWS, ("z", "c"))
    return jax.shard_map(local, mesh=fine, in_specs=in_specs, out_specs=out_specs, check_vma=False)
```

profile of v0, /device:TPU:32, one launch (start us, length us, event | category | flops | bytes accessed | tf_op | source)
XLA Modules:
  0.0 125.4 jit_solution(3803489945724805696)
XLA Ops:
  0.5 0.9 constant_dynamic-slice_fusion
  1.4 1.9 %collective-permute-start.2 = (f32[2,128,128]{2,1,0:T(8,128)S(1)}, f32[2,128,128]{2,1,0:T(8,128)S(1)}, u32[]{:S(2)}, u32[]{:S(2)}) collective-permute-start(f32[2,128,128]{2,1,0:T(8,128)S(1)} %constant_dynamic-slice_fusion), channel_id=1, source_target_pairs={{0,2},{2,0},{4,6},{6,4},{1,3},{3,1},{5,7},{7,5},{8,10},{10,8},{12,... | collective-permute-start | bytes 393224 | tf_op jit(solution)/shard_map/ppermute | solution.py:201
  5.6 1.5 %collective-permute-done.2.after.own = f32[2,128,128]{2,1,0:T(8,128)S(1)} collective-permute-done((f32[2,128,128]{2,1,0:T(8,128)S(1)}, f32[2,128,128]{2,1,0:T(8,128)S(1)}, u32[]{:S(2)}, u32[]{:S(2)}) %collective-permute-start.2) | collective-permute-done | bytes 131104 | tf_op jit(solution)/shard_map/ppermute | solution.py:201
  7.0 1.5 %collective-permute-start.7 = (f32[2,128,128]{2,1,0:T(8,128)S(1)}, f32[2,128,128]{2,1,0:T(8,128)S(1)}, u32[]{:S(2)}, u32[]{:S(2)}) collective-permute-start(f32[2,128,128]{2,1,0:T(8,128)S(1)} %collective-permute-done.2.after.own), channel_id=1, source_target_pairs={{0,8},{8,16},{16,24},{24,0},{1,9},{9,17},{17,25},{25,1},{2,10},{10... | collective-permute-start | bytes 393224 | tf_op jit(solution)/shard_map/ppermute | solution.py:193
  8.5 1.8 %collective-permute-start.8 = (f32[2,128,128]{2,1,0:T(8,128)S(1)}, f32[2,128,128]{2,1,0:T(8,128)S(1)}, u32[]{:S(2)}, u32[]{:S(2)}) collective-permute-start(f32[2,128,128]{2,1,0:T(8,128)S(1)} %collective-permute-done.2.after.own), channel_id=1, source_target_pairs={{0,24},{8,0},{16,8},{24,16},{1,25},{9,1},{17,9},{25,17},{2,26},{10... | collective-permute-start | bytes 393224 | tf_op jit(solution)/shard_map/ppermute | solution.py:193
  10.3 1.8 %collective-permute-start.9 = (f32[2,128,128]{2,1,0:T(8,128)S(1)}, f32[2,128,128]{2,1,0:T(8,128)S(1)}, u32[]{:S(2)}, u32[]{:S(2)}) collective-permute-start(f32[2,128,128]{2,1,0:T(8,128)S(1)} %collective-permute-done.2.after.own), channel_id=1, source_target_pairs={{0,16},{8,24},{16,0},{24,8},{1,17},{9,25},{17,1},{25,9},{2,18},{10... | collective-permute-start | bytes 393224 | tf_op jit(solution)/shard_map/ppermute | solution.py:193
  12.1 0.7 compare_select_fusion.3
  13.3 1.4 %collective-permute-done.8.up = f32[2,128,128]{2,1,0:T(8,128)S(1)} collective-permute-done((f32[2,128,128]{2,1,0:T(8,128)S(1)}, f32[2,128,128]{2,1,0:T(8,128)S(1)}, u32[]{:S(2)}, u32[]{:S(2)}) %collective-permute-start.8) | collective-permute-done | bytes 131104 | tf_op jit(solution)/shard_map/ppermute | solution.py:193
  14.7 2.3 %collective-permute-done.9.far = f32[2,128,128]{2,1,0:T(8,128)S(1)} collective-permute-done((f32[2,128,128]{2,1,0:T(8,128)S(1)}, f32[2,128,128]{2,1,0:T(8,128)S(1)}, u32[]{:S(2)}, u32[]{:S(2)}) %collective-permute-start.9) | collective-permute-done | bytes 131104 | tf_op jit(solution)/shard_map/ppermute | solution.py:193
  17.6 1.7 %collective-permute-start.10 = (f32[8,128,128]{2,1,0:T(8,128)S(1)}, f32[8,128,128]{2,1,0:T(8,128)}, u32[]{:S(2)}, u32[]{:S(2)}) collective-permute-start(f32[8,128,128]{2,1,0:T(8,128)S(1)} %join_kernel.1.refs_0_), channel_id=1, source_target_pairs={{0,64},{64,128},{128,192},{192,0},{1,65},{65,129},{129,193},{193,1... | collective-permute-start | bytes 1572872 | tf_op jit(solution)/shard_map/ppermute | solution.py:193
  19.2 1.7 %collective-permute-start.11 = (f32[8,128,128]{2,1,0:T(8,128)S(1)}, f32[8,128,128]{2,1,0:T(8,128)}, u32[]{:S(2)}, u32[]{:S(2)}) collective-permute-start(f32[8,128,128]{2,1,0:T(8,128)S(1)} %join_kernel.1.refs_0_), channel_id=1, source_target_pairs={{0,192},{64,0},{128,64},{192,128},{1,193},{65,1},{129,65},{193,129... | collective-permute-start | bytes 1572872 | tf_op jit(solution)/shard_map/ppermute | solution.py:193
  20.9 0.9 copy-done.1
  21.8 0.9 turn_kernel.1
  22.8 12.7 %all-to-all-start = ((f32[128,8,128]{2,1,0:T(8,128)}), f32[128,8,128]{2,1,0:T(8,128)S(1)}, u32[]{:S(2)}, u32[]{:S(2)}) async-start(f32[128,8,128]{2,1,0:T(8,128)} %bitcast.8), calls=%async_computation | async-start | bytes 1048576 | tf_op jit(solution)/shard_map/all_to_all | solution.py:246
  35.5 1.5 %collective-permute-start.4 = (f32[128,512]{1,0:T(8,128)S(1)}, f32[128,512]{1,0:T(8,128)S(1)}, u32[]{:S(2)}, u32[]{:S(2)}) collective-permute-start(f32[128,512]{1,0:T(8,128)S(1)} %copy-done.2), channel_id=1, source_target_pairs={{0,2},{2,4},{4,6},{6,0},{1,3},{3,5},{5,7},{7,1},{8,10},{10,12},{12... | collective-permute-start | bytes 786440 | tf_op jit(solution)/shard_map/ppermute | solution.py:193
  37.1 1.8 %collective-permute-start.5 = (f32[128,512]{1,0:T(8,128)S(1)}, f32[128,512]{1,0:T(8,128)S(1)}, u32[]{:S(2)}, u32[]{:S(2)}) collective-permute-start(f32[128,512]{1,0:T(8,128)S(1)} %copy-done.2), channel_id=1, source_target_pairs={{0,4},{2,6},{4,0},{6,2},{1,5},{3,7},{5,1},{7,3},{8,12},{10,14},{12... | collective-permute-start | bytes 786440 | tf_op jit(solution)/shard_map/ppermute | solution.py:193
  38.9 1.1 collective-permute-start.6
  40.0 1.0 slice.8
  41.0 1.7 %collective-permute-start.12 = (f32[4,128,128]{2,1,0:T(8,128)S(1)}, f32[4,128,128]{2,1,0:T(8,128)}, u32[]{:S(2)}, u32[]{:S(2)}) collective-permute-start(f32[4,128,128]{2,1,0:T(8,128)S(1)} %slice.8), channel_id=1, source_target_pairs={{0,64},{64,128},{128,192},{192,0},{1,65},{65,129},{129,193},{193,1... | collective-permute-start | bytes 786440 | tf_op jit(solution)/shard_map/ppermute | solution.py:193
  42.6 1.0 slice.9
  43.6 18.4 %collective-permute-done.4.w1 = f32[128,512]{1,0:T(8,128)S(1)} collective-permute-done((f32[128,512]{1,0:T(8,128)S(1)}, f32[128,512]{1,0:T(8,128)S(1)}, u32[]{:S(2)}, u32[]{:S(2)}) %collective-permute-start.4) | collective-permute-done | bytes 262176 | tf_op jit(solution)/shard_map/ppermute | solution.py:193
  62.7 2.8 %collective-permute-start.13 = (f32[4,128,128]{2,1,0:T(8,128)S(1)}, f32[4,128,128]{2,1,0:T(8,128)}, u32[]{:S(2)}, u32[]{:S(2)}) collective-permute-start(f32[4,128,128]{2,1,0:T(8,128)S(1)} %slice.9), channel_id=1, source_target_pairs={{0,192},{64,0},{128,64},{192,128},{1,193},{65,1},{129,65},{193,129... | collective-permute-start | bytes 786440 | tf_op jit(solution)/shard_map/ppermute | solution.py:193
  66.7 1.2 collective-permute-done.6.w3
  69.9 5.3 %alpha_near_kernel.1 = (f32[32,32,128]{2,1,0:T(8,128)S(1)}, bf16[32,64,128]{2,1,0:T(8,128)(2,1)S(1)}) custom-call(s32[128]{0:T(128)S(1)} %get-tuple-element.24.cols, s32[128]{0:T(128)S(1)} %convert_reduce_fusion.owners, f32[32,32,128]{2,1,0:T(8,128)S(1)} %bitcast.12, f32[32,128,128]{2,1,0:T(8,128)S(1)} %copy-done, f32[32,128,128]{2,1,0:T(8,128)} %collective-permute-done.3.h1), custom_call_target="tpu_custom_call" | custom-call | flops 402653184 | bytes 7340032 | tf_op jit(solution)/shard_map/alpha_near_kernel/pallas_call | solution.py:226
  75.3 5.2 %beta_near_kernel.1 = (f32[16,128,128]{2,1,0:T(8,128)S(1)}, bf16[16,256,128]{2,1,0:T(8,128)(2,1)S(1)}) custom-call(s32[4]{0:T(128)S(1)} %pad_add_fusion.where, s32[128]{0:T(128)S(1)} %get-tuple-element.24.cols, s32[128]{0:T(128)S(1)} %get-tuple-element.23.slots, f32[128,512]{1,0:T(8,128)S(1)} %copy-done.2, f32[128,512]{1,0:T(8,128)S(1)} %copy-done.4, ...), custom_call_target="tpu_custom_call" | custom-call | flops 402653184 | bytes 7340032 | tf_op jit(solution)/shard_map/beta_near_kernel/pallas_call | solution.py:226
  80.6 7.0 %far_kernel.1 = (f32[32,32,128]{2,1,0:T(8,128)}, f32[8,128,128]{2,1,0:T(8,128)S(1)}, f32[8,128,128]{2,1,0:T(8,128)S(1)}) custom-call(s32[4]{0:T(128)S(1)} %pad_add_fusion.where, s32[128]{0:T(128)S(1)} %get-tuple-element.24.cols, s32[128]{0:T(128)S(1)} %convert_reduce_fusion.owners, s32[128]{0:T(128)S(1)} %get-tuple-element.23.slots, ...), custom_call_target="tpu_custom_call" | custom-call | flops 402653184 | bytes 8388608 | tf_op jit(solution)/shard_map/far_kernel/pallas_call | solution.py:226
  87.5 16.6 %all-to-all-start.1 = ((f32[128,8,128]{2,1,0:T(8,128)}), f32[128,8,128]{2,1,0:T(8,128)S(1)}, u32[]{:S(2)}, u32[]{:S(2)}) async-start(f32[128,8,128]{2,1,0:T(8,128)} %bitcast.10), calls=%async_computation.1 | async-start | bytes 1048576 | tf_op jit(solution)/shard_map/all_to_all | solution.py:298
  104.2 1.9 %collective-permute-done.19.got_ref = f32[8,128,128]{2,1,0:T(8,128)S(1)} collective-permute-done((f32[8,128,128]{2,1,0:T(8,128)S(1)}, f32[8,128,128]{2,1,0:T(8,128)S(1)}, u32[]{:S(2)}, u32[]{:S(2)}) %collective-permute-start.19) | collective-permute-done | bytes 524320 | tf_op jit(solution)/shard_map/ppermute | solution.py:197
  106.2 3.4 %collective-permute-start.20 = (f32[4,128,128]{2,1,0:T(8,128)S(1)}, f32[4,128,128]{2,1,0:T(8,128)S(1)}, u32[]{:S(2)}, u32[]{:S(2)}) collective-permute-start(f32[4,128,128]{2,1,0:T(8,128)S(1)} %get-tuple-element.22), channel_id=1, source_target_pairs={{2,4},{4,2},{3,5},{5,3},{10,12},{12,10},{11,13},{13,11},{18,20},{2... | collective-permute-start | bytes 786440 | tf_op jit(solution)/shard_map/ppermute | solution.py:300
  109.6 12.8 %collective-permute-done.20.got_ref = f32[4,128,128]{2,1,0:T(8,128)S(1)} collective-permute-done((f32[4,128,128]{2,1,0:T(8,128)S(1)}, f32[4,128,128]{2,1,0:T(8,128)S(1)}, u32[]{:S(2)}, u32[]{:S(2)}) %collective-permute-start.20) | collective-permute-done | bytes 262176 | tf_op jit(solution)/shard_map/ppermute | solution.py:300
  122.3 2.2 %all-to-all-done.1 = f32[128,8,128]{2,1,0:T(8,128)S(1)} async-done(((f32[128,8,128]{2,1,0:T(8,128)}), f32[128,8,128]{2,1,0:T(8,128)S(1)}, u32[]{:S(2)}, u32[]{:S(2)}) %all-to-all-start.1) | async-done | bytes 524320 | tf_op jit(solution)/shard_map/all_to_all | solution.py:298
  124.5 0.8 final_kernel.1
  (50 shorter events, 7.9 us)
Async XLA Ops:
  0.0 35.5 %copy-start.2 = (f32[128,512]{1,0:T(8,128)S(1)}, f32[128,512]{1,0:T(8,128)}, u32[]{:S(2)}) copy-start(f32[128,512]{1,0:T(8,128)} %w0.1) | copy-start | bytes 786436
  0.0 4.5 %collective-permute-start = (s32[32]{0:T(128)}, s32[32]{0:T(128)S(1)}, u32[]{:S(2)}, u32[]{:S(2)}) collective-permute-start(s32[32]{0:T(128)} %param.7), channel_id=1, source_target_pairs={{0,1},{1,0},{2,3},{3,2},{4,5},{5,4},{6,7},{7,6},{8,9},{9,8},{10,11... | collective-permute-start | bytes 392 | tf_op jit(solution)/shard_map/ppermute | solution.py:197
  0.0 69.4 %collective-permute-start.3 = (f32[32,128,128]{2,1,0:T(8,128)}, f32[32,128,128]{2,1,0:T(8,128)}, u32[]{:S(2)}, u32[]{:S(2)}) collective-permute-start(f32[32,128,128]{2,1,0:T(8,128)} %h0.3), channel_id=1, source_target_pairs={{0,1},{1,0},{2,3},{3,2},{4,5},{5,4},{6,7},{7,6},{8,9},{9,8},{10,11... | collective-permute-start | bytes 6291464 | tf_op jit(solution)/shard_map/ppermute | solution.py:197
  1.4 68.5 %copy-start = (f32[32,128,128]{2,1,0:T(8,128)S(1)}, f32[32,128,128]{2,1,0:T(8,128)}, u32[]{:S(2)}) copy-start(f32[32,128,128]{2,1,0:T(8,128)} %h0.3) | copy-start | bytes 6291460
  1.4 5.6 %collective-permute-start.2 = (f32[2,128,128]{2,1,0:T(8,128)S(1)}, f32[2,128,128]{2,1,0:T(8,128)S(1)}, u32[]{:S(2)}, u32[]{:S(2)}) collective-permute-start(f32[2,128,128]{2,1,0:T(8,128)S(1)} %constant_dynamic-slice_fusion), channel_id=1, source_target_pairs={{0,2},{2,0},{4,6},{6,4},{1,3},{3,1},{5,7},{7,5},{8,10},{10,8},{12,... | collective-permute-start | bytes 393224 | tf_op jit(solution)/shard_map/ppermute | solution.py:201
  5.3 6.8 %collective-permute-start.1 = (s32[64]{0:T(128)S(1)}, s32[64]{0:T(128)S(1)}, u32[]{:S(2)}, u32[]{:S(2)}) collective-permute-start(s32[64]{0:T(128)S(1)} %pad_add_fusion.1), channel_id=1, source_target_pairs={{0,2},{2,0},{4,6},{6,4},{1,3},{3,1},{5,7},{7,5},{8,10},{10,8},{12,... | collective-permute-start | bytes 776 | tf_op jit(solution)/shard_map/ppermute | solution.py:201
  7.0 6.3 %collective-permute-start.7 = (f32[2,128,128]{2,1,0:T(8,128)S(1)}, f32[2,128,128]{2,1,0:T(8,128)S(1)}, u32[]{:S(2)}, u32[]{:S(2)}) collective-permute-start(f32[2,128,128]{2,1,0:T(8,128)S(1)} %collective-permute-done.2.after.own), channel_id=1, source_target_pairs={{0,8},{8,16},{16,24},{24,0},{1,9},{9,17},{17,25},{25,1},{2,10},{10... | collective-permute-start | bytes 393224 | tf_op jit(solution)/shard_map/ppermute | solution.py:193
  8.5 6.2 %collective-permute-start.8 = (f32[2,128,128]{2,1,0:T(8,128)S(1)}, f32[2,128,128]{2,1,0:T(8,128)S(1)}, u32[]{:S(2)}, u32[]{:S(2)}) collective-permute-start(f32[2,128,128]{2,1,0:T(8,128)S(1)} %collective-permute-done.2.after.own), channel_id=1, source_target_pairs={{0,24},{8,0},{16,8},{24,16},{1,25},{9,1},{17,9},{25,17},{2,26},{10... | collective-permute-start | bytes 393224 | tf_op jit(solution)/shard_map/ppermute | solution.py:193
  10.3 6.7 %collective-permute-start.9 = (f32[2,128,128]{2,1,0:T(8,128)S(1)}, f32[2,128,128]{2,1,0:T(8,128)S(1)}, u32[]{:S(2)}, u32[]{:S(2)}) collective-permute-start(f32[2,128,128]{2,1,0:T(8,128)S(1)} %collective-permute-done.2.after.own), channel_id=1, source_target_pairs={{0,16},{8,24},{16,0},{24,8},{1,17},{9,25},{17,1},{25,9},{2,18},{10... | collective-permute-start | bytes 393224 | tf_op jit(solution)/shard_map/ppermute | solution.py:193
  17.6 21.3 %collective-permute-start.10 = (f32[8,128,128]{2,1,0:T(8,128)S(1)}, f32[8,128,128]{2,1,0:T(8,128)}, u32[]{:S(2)}, u32[]{:S(2)}) collective-permute-start(f32[8,128,128]{2,1,0:T(8,128)S(1)} %join_kernel.1.refs_0_), channel_id=1, source_target_pairs={{0,64},{64,128},{128,192},{192,0},{1,65},{65,129},{129,193},{193,1... | collective-permute-start | bytes 1572872 | tf_op jit(solution)/shard_map/ppermute | solution.py:193
  19.2 21.7 %collective-permute-start.11 = (f32[8,128,128]{2,1,0:T(8,128)S(1)}, f32[8,128,128]{2,1,0:T(8,128)}, u32[]{:S(2)}, u32[]{:S(2)}) collective-permute-start(f32[8,128,128]{2,1,0:T(8,128)S(1)} %join_kernel.1.refs_0_), channel_id=1, source_target_pairs={{0,192},{64,0},{128,64},{192,128},{1,193},{65,1},{129,65},{193,129... | collective-permute-start | bytes 1572872 | tf_op jit(solution)/shard_map/ppermute | solution.py:193
  20.9 0.9 copy-start.1
  22.8 47.1 %all-to-all-start = ((f32[128,8,128]{2,1,0:T(8,128)}), f32[128,8,128]{2,1,0:T(8,128)S(1)}, u32[]{:S(2)}, u32[]{:S(2)}) async-start(f32[128,8,128]{2,1,0:T(8,128)} %bitcast.8), calls=%async_computation | async-start | bytes 1048576 | tf_op jit(solution)/shard_map/all_to_all | solution.py:246
  35.5 26.5 %collective-permute-start.4 = (f32[128,512]{1,0:T(8,128)S(1)}, f32[128,512]{1,0:T(8,128)S(1)}, u32[]{:S(2)}, u32[]{:S(2)}) collective-permute-start(f32[128,512]{1,0:T(8,128)S(1)} %copy-done.2), channel_id=1, source_target_pairs={{0,2},{2,4},{4,6},{6,0},{1,3},{3,5},{5,7},{7,1},{8,10},{10,12},{12... | collective-permute-start | bytes 786440 | tf_op jit(solution)/shard_map/ppermute | solution.py:193
  37.1 28.9 %collective-permute-start.5 = (f32[128,512]{1,0:T(8,128)S(1)}, f32[128,512]{1,0:T(8,128)S(1)}, u32[]{:S(2)}, u32[]{:S(2)}) collective-permute-start(f32[128,512]{1,0:T(8,128)S(1)} %copy-done.2), channel_id=1, source_target_pairs={{0,4},{2,6},{4,0},{6,2},{1,5},{3,7},{5,1},{7,3},{8,12},{10,14},{12... | collective-permute-start | bytes 786440 | tf_op jit(solution)/shard_map/ppermute | solution.py:193
  38.9 29.0 %collective-permute-start.6 = (f32[128,512]{1,0:T(8,128)S(1)}, f32[128,512]{1,0:T(8,128)S(1)}, u32[]{:S(2)}, u32[]{:S(2)}) collective-permute-start(f32[128,512]{1,0:T(8,128)S(1)} %copy-done.2), channel_id=1, source_target_pairs={{0,6},{2,0},{4,2},{6,4},{1,7},{3,1},{5,3},{7,5},{8,14},{10,8},{12,... | collective-permute-start | bytes 786440 | tf_op jit(solution)/shard_map/ppermute | solution.py:193
  41.0 27.6 %collective-permute-start.12 = (f32[4,128,128]{2,1,0:T(8,128)S(1)}, f32[4,128,128]{2,1,0:T(8,128)}, u32[]{:S(2)}, u32[]{:S(2)}) collective-permute-start(f32[4,128,128]{2,1,0:T(8,128)S(1)} %slice.8), channel_id=1, source_target_pairs={{0,64},{64,128},{128,192},{192,0},{1,65},{65,129},{129,193},{193,1... | collective-permute-start | bytes 786440 | tf_op jit(solution)/shard_map/ppermute | solution.py:193
  62.0 0.7 copy-start.3
  62.7 6.7 %collective-permute-start.13 = (f32[4,128,128]{2,1,0:T(8,128)S(1)}, f32[4,128,128]{2,1,0:T(8,128)}, u32[]{:S(2)}, u32[]{:S(2)}) collective-permute-start(f32[4,128,128]{2,1,0:T(8,128)S(1)} %slice.9), channel_id=1, source_target_pairs={{0,192},{64,0},{128,64},{192,128},{1,193},{65,1},{129,65},{193,129... | collective-permute-start | bytes 786440 | tf_op jit(solution)/shard_map/ppermute | solution.py:193
  65.9 0.7 copy-start.5
  66.7 13.9 %collective-permute-start.14 = (f32[8,128,128]{2,1,0:T(8,128)S(1)}, f32[8,128,128]{2,1,0:T(8,128)}, u32[]{:S(2)}, u32[]{:S(2)}) collective-permute-start(f32[8,128,128]{2,1,0:T(8,128)S(1)} %join_kernel.1.refs_0_), channel_id=1, source_target_pairs={{0,1},{1,0},{2,3},{3,2},{4,5},{5,4},{6,7},{7,6},{8,9},{9,8},{10,11... | collective-permute-start | bytes 1572872 | tf_op jit(solution)/shard_map/ppermute | solution.py:197
  67.9 0.7 copy-start.7
  68.6 12.0 %collective-permute-start.15 = (f32[8,128,128]{2,1,0:T(8,128)}, f32[8,128,128]{2,1,0:T(8,128)}, u32[]{:S(2)}, u32[]{:S(2)}) collective-permute-start(f32[8,128,128]{2,1,0:T(8,128)} %collective-permute-done.10.refs_1_), channel_id=1, source_target_pairs={{0,1},{1,0},{2,3},{3,2},{4,5},{5,4},{6,7},{7,6},{8,9},{9,8},{10,11... | collective-permute-start | bytes 1572872 | tf_op jit(solution)/shard_map/ppermute | solution.py:197
  68.6 12.0 %collective-permute-start.16 = (f32[8,128,128]{2,1,0:T(8,128)}, f32[8,128,128]{2,1,0:T(8,128)}, u32[]{:S(2)}, u32[]{:S(2)}) collective-permute-start(f32[8,128,128]{2,1,0:T(8,128)} %collective-permute-done.11.refs_2_), channel_id=1, source_target_pairs={{0,1},{1,0},{2,3},{3,2},{4,5},{5,4},{6,7},{7,6},{8,9},{9,8},{10,11... | collective-permute-start | bytes 1572872 | tf_op jit(solution)/shard_map/ppermute | solution.py:197
  69.4 11.1 %collective-permute-start.17 = (f32[4,128,128]{2,1,0:T(8,128)}, f32[4,128,128]{2,1,0:T(8,128)}, u32[]{:S(2)}, u32[]{:S(2)}) collective-permute-start(f32[4,128,128]{2,1,0:T(8,128)} %collective-permute-done.12.refs_3_), channel_id=1, source_target_pairs={{0,1},{1,0},{2,3},{3,2},{4,5},{5,4},{6,7},{7,6},{8,9},{9,8},{10,11... | collective-permute-start | bytes 786440 | tf_op jit(solution)/shard_map/ppermute | solution.py:197
  69.4 11.1 %collective-permute-start.18 = (f32[4,128,128]{2,1,0:T(8,128)}, f32[4,128,128]{2,1,0:T(8,128)}, u32[]{:S(2)}, u32[]{:S(2)}) collective-permute-start(f32[4,128,128]{2,1,0:T(8,128)} %collective-permute-done.13.refs_4_), channel_id=1, source_target_pairs={{0,1},{1,0},{2,3},{3,2},{4,5},{5,4},{6,7},{7,6},{8,9},{9,8},{10,11... | collective-permute-start | bytes 786440 | tf_op jit(solution)/shard_map/ppermute | solution.py:197
  69.9 5.4 %copy-start.4 = (f32[128,512]{1,0:T(8,128)S(1)}, f32[128,512]{1,0:T(8,128)}, u32[]{:S(2)}) copy-start(f32[128,512]{1,0:T(8,128)} %copy-done.3) | copy-start | bytes 786436
  69.9 5.4 %copy-start.6 = (f32[128,512]{1,0:T(8,128)S(1)}, f32[128,512]{1,0:T(8,128)}, u32[]{:S(2)}) copy-start(f32[128,512]{1,0:T(8,128)} %copy-done.5) | copy-start | bytes 786436
  69.9 5.4 %copy-start.8 = (f32[128,512]{1,0:T(8,128)S(1)}, f32[128,512]{1,0:T(8,128)}, u32[]{:S(2)}) copy-start(f32[128,512]{1,0:T(8,128)} %copy-done.7) | copy-start | bytes 786436
  87.5 37.0 %all-to-all-start.1 = ((f32[128,8,128]{2,1,0:T(8,128)}), f32[128,8,128]{2,1,0:T(8,128)S(1)}, u32[]{:S(2)}, u32[]{:S(2)}) async-start(f32[128,8,128]{2,1,0:T(8,128)} %bitcast.10), calls=%async_computation.1 | async-start | bytes 1048576 | tf_op jit(solution)/shard_map/all_to_all | solution.py:298
  104.1 2.0 %collective-permute-start.19 = (f32[8,128,128]{2,1,0:T(8,128)S(1)}, f32[8,128,128]{2,1,0:T(8,128)S(1)}, u32[]{:S(2)}, u32[]{:S(2)}) collective-permute-start(f32[8,128,128]{2,1,0:T(8,128)S(1)} %get-tuple-element.20), channel_id=1, source_target_pairs={{0,1},{1,0},{2,3},{3,2},{4,5},{5,4},{6,7},{7,6},{8,9},{9,8},{10,11... | collective-permute-start | bytes 1572872 | tf_op jit(solution)/shard_map/ppermute | solution.py:197
  106.2 16.1 %collective-permute-start.20 = (f32[4,128,128]{2,1,0:T(8,128)S(1)}, f32[4,128,128]{2,1,0:T(8,128)S(1)}, u32[]{:S(2)}, u32[]{:S(2)}) collective-permute-start(f32[4,128,128]{2,1,0:T(8,128)S(1)} %get-tuple-element.22), channel_id=1, source_target_pairs={{2,4},{4,2},{3,5},{5,3},{10,12},{12,10},{11,13},{13,11},{18,20},{2... | collective-permute-start | bytes 786440 | tf_op jit(solution)/shard_map/ppermute | solution.py:300
where the time goes:
time: 126 us; the launch traced here: 125 us
  starting transfers between devices  53.8 us (43%)
  waiting for transfers between devices  42.9 us (34%)
  Pallas kernels  19.9 us (16%)
  local copies, waits for them, and re-layouts  6.05 us (5%)
  other arithmetic  2.55 us (2%)
    ppermute x10, waiting for transfers between devices, shift(): return lax.ppermute(value, axis, [(i, (i + by) % 4) for i in range(4)])  24.5 us
    pallas_call x7, Pallas kernels, call(): pl.pallas_call(kernel, out_shape=outs, in_specs=in_specs, out_specs=VMEM...  19.9 us
    ppermute x10, starting transfers between devices, shift(): return lax.ppermute(value, axis, [(i, (i + by) % 4) for i in range(4)])  17.3 us
    all_to_all x1, starting transfers between devices, local(): lax.all_to_all(out_a.reshape(1024, 128), ROWS + ('z',), 0, 0, tiled=True)  16.6 us
    ppermute x1, waiting for transfers between devices, local(): got = lax.ppermute(other, 'z', [(1, 2), (2, 1)])  12.8 us
    all_to_all x1, starting transfers between devices, local(): lax.all_to_all(at.reshape(1024, 128), ROWS + ('z',), 0, 0, tiled=True)  12.7 us
    ppermute x1, starting transfers between devices, local(): got = lax.ppermute(other, 'z', [(1, 2), (2, 1)])  3.37 us
    unnamed x18, local copies, waits for them, and re-layouts  3.11 us
  transfers between devices with their start and end apart: 23, of which 11 were waited for; matrix products, arithmetic and copies ran while one was open for 4% of the time, Pallas kernels for 10%

commit v1 on v0

--- a/solution.py
+++ b/solution.py
@@ -28,7 +28,7 @@
     return jax.ShapeDtypeStruct(dims, kind)
 
 
-def turn_kernel(c_ref, after, at_ref):
+def turn_kernel(c_ref, w1, w2, w3, at_ref):
     for t in range(4):
         turned = jnp.transpose(c_ref[:, 128 * t : 128 * (t + 1)]).reshape(8, 16, 128)
         at_ref[8 * t : 8 * (t + 1), 0] = turned
@@ -242,9 +242,9 @@
 
     near_swapped = swap(hblocks)
     piece = pair(lax.dynamic_slice_in_dim(hblocks, 2 * (4 * y + x), 2, axis=0))
-    at = call(turn_kernel, shape(32, 2, 16, 128), [VMEM, ANY], coeffs, piece)
+    rows = [coeffs] + [shift(coeffs, "z", k) for k in (1, 2, 3)]
+    at = call(turn_kernel, shape(32, 2, 16, 128), [VMEM] + [ANY] * 3, *rows)
     moved = lax.all_to_all(at.reshape(1024, 128), ROWS + ("z",), 0, 0, tiled=True)
-    rows = [coeffs] + [shift(coeffs, "z", k) for k in (1, 2, 3)]
     joined = call(
         join_kernel, shape(8, 128, 128), [SMEM] * 2 + [VMEM] * 4,
         where, cols, piece, *(shift(piece, "x", by) for by in (1, -1, 2)),

time: 126 us -> 142 us (1.13)
  waiting for transfers between devices: 42.9 us -> 56.1 us
  local copies, waits for them, and re-layouts: 6.05 us -> 8.73 us
    ppermute x2, waiting for transfers between devices: 1.49 us -> 8.88 us  [pair(): return lax.ppermute(value, 'z', [(0, 1), (1, 0), (2, 3), (3, 2)])]
    ppermute x10, waiting for transfers between devices: 24.5 us -> 31.1 us  [shift(): return lax.ppermute(value, axis, [(i, (i + by) % 4) for i in range(4)])]
    unnamed x18 -> x26, local copies, waits for them, and re-layouts: 3.11 us -> 5.8 us
  transfers between devices with their start and end apart: 23 -> 23, of which waited for: 11 -> 10; matrix products, arithmetic and copies ran while one was open for 4% -> 4% of each run, Pallas kernels for 10% -> 8%
where the time goes in v1:
time: 142 us
  waiting for transfers between devices  56.1 us (40%)
  starting transfers between devices  55.1 us (39%)
  Pallas kernels  19.4 us (14%)
  local copies, waits for them, and re-layouts  8.73 us (6%)
  other arithmetic  2.54 us (2%)
    ppermute x10, waiting for transfers between devices, shift(): return lax.ppermute(value, axis, [(i, (i + by) % 4) for i in range(4)])  31.1 us
    pallas_call x7, Pallas kernels, call(): pl.pallas_call(kernel, out_shape=outs, in_specs=in_specs, out_specs=VMEM...  19.4 us
    ppermute x10, starting transfers between devices, shift(): return lax.ppermute(value, axis, [(i, (i + by) % 4) for i in range(4)])  17.9 us
    all_to_all x1, starting transfers between devices, local(): lax.all_to_all(out_a.reshape(1024, 128), ROWS + ('z',), 0, 0, tiled=True)  16.2 us
    all_to_all x1, starting transfers between devices, local(): lax.all_to_all(at.reshape(1024, 128), ROWS + ('z',), 0, 0, tiled=True)  13.3 us
    ppermute x1, waiting for transfers between devices, local(): got = lax.ppermute(other, 'z', [(1, 2), (2, 1)])  11.8 us
    ppermute x2, waiting for transfers between devices, pair(): return lax.ppermute(value, 'z', [(0, 1), (1, 0), (2, 3), (3, 2)])  8.88 us
    unnamed x26, local copies, waits for them, and re-layouts  5.8 us
  transfers between devices with their start and end apart: 23, of which 10 were waited for; matrix products, arithmetic and copies ran while one was open for 4% of the time, Pallas kernels for 8%

profile of v1, /device:TPU:32, one launch (start us, length us, event | category | flops | bytes accessed | tf_op | source)
XLA Modules:
  0.0 142.1 jit_solution(16492427404872945471)
XLA Ops:
  0.5 1.9 %collective-permute-start.2 = (f32[128,512]{1,0:T(8,128)}, f32[128,512]{1,0:T(8,128)S(1)}, u32[]{:S(2)}, u32[]{:S(2)}) collective-permute-start(f32[128,512]{1,0:T(8,128)} %w0.1), channel_id=1, source_target_pairs={{0,2},{2,4},{4,6},{6,0},{1,3},{3,5},{5,7},{7,1},{8,10},{10,12},{12... | collective-permute-start | bytes 786440 | tf_op jit(solution)/shard_map/ppermute | solution.py:193
  4.6 7.4 %collective-permute-done.6.own = f32[2,128,128]{2,1,0:T(8,128)S(1)} collective-permute-done((f32[2,128,128]{2,1,0:T(8,128)S(1)}, f32[2,128,128]{2,1,0:T(8,128)S(1)}, u32[]{:S(2)}, u32[]{:S(2)}) %collective-permute-start.6) | collective-permute-done | bytes 131104 | tf_op jit(solution)/shard_map/ppermute | solution.py:201
  12.0 1.5 %collective-permute-start.7 = (f32[2,128,128]{2,1,0:T(8,128)S(1)}, f32[2,128,128]{2,1,0:T(8,128)S(1)}, u32[]{:S(2)}, u32[]{:S(2)}) collective-permute-start(f32[2,128,128]{2,1,0:T(8,128)S(1)} %collective-permute-done.6.own), channel_id=1, source_target_pairs={{0,8},{8,16},{16,24},{24,0},{1,9},{9,17},{17,25},{25,1},{2,10},{10... | collective-permute-start | bytes 393224 | tf_op jit(solution)/shard_map/ppermute | solution.py:193
  13.5 1.7 %collective-permute-start.8 = (f32[2,128,128]{2,1,0:T(8,128)S(1)}, f32[2,128,128]{2,1,0:T(8,128)S(1)}, u32[]{:S(2)}, u32[]{:S(2)}) collective-permute-start(f32[2,128,128]{2,1,0:T(8,128)S(1)} %collective-permute-done.6.own), channel_id=1, source_target_pairs={{0,24},{8,0},{16,8},{24,16},{1,25},{9,1},{17,9},{25,17},{2,26},{10... | collective-permute-start | bytes 393224 | tf_op jit(solution)/shard_map/ppermute | solution.py:193
  16.0 2.5 %collective-permute-start.1 = (s32[64]{0:T(128)S(1)}, s32[64]{0:T(128)S(1)}, u32[]{:S(2)}, u32[]{:S(2)}) collective-permute-start(s32[64]{0:T(128)S(1)} %pad_add_fusion.1), channel_id=1, source_target_pairs={{0,2},{2,0},{4,6},{6,4},{1,3},{3,1},{5,7},{7,5},{8,10},{10,8},{12,... | collective-permute-start | bytes 776 | tf_op jit(solution)/shard_map/ppermute | solution.py:201
  18.5 1.5 %collective-permute-done.1 = s32[64]{0:T(128)S(1)} collective-permute-done((s32[64]{0:T(128)S(1)}, s32[64]{0:T(128)S(1)}, u32[]{:S(2)}, u32[]{:S(2)}) %collective-permute-start.1) | collective-permute-done | bytes 288 | tf_op jit(solution)/shard_map/ppermute | solution.py:201
  20.0 2.6 %collective-permute-start.3 = (f32[128,512]{1,0:T(8,128)}, f32[128,512]{1,0:T(8,128)S(1)}, u32[]{:S(2)}, u32[]{:S(2)}) collective-permute-start(f32[128,512]{1,0:T(8,128)} %w0.1), channel_id=1, source_target_pairs={{0,4},{2,6},{4,0},{6,2},{1,5},{3,7},{5,1},{7,3},{8,12},{10,14},{12... | collective-permute-start | bytes 786440 | tf_op jit(solution)/shard_map/ppermute | solution.py:193
  23.5 1.2 collective-permute-start.9
  25.5 4.6 %collective-permute-done.9.far = f32[2,128,128]{2,1,0:T(8,128)S(1)} collective-permute-done((f32[2,128,128]{2,1,0:T(8,128)S(1)}, f32[2,128,128]{2,1,0:T(8,128)S(1)}, u32[]{:S(2)}, u32[]{:S(2)}) %collective-permute-start.9) | collective-permute-done | bytes 131104 | tf_op jit(solution)/shard_map/ppermute | solution.py:193
  30.6 1.0 collective-permute-start.10
  31.6 6.0 %collective-permute-done.3.w2 = f32[128,512]{1,0:T(8,128)S(1)} collective-permute-done((f32[128,512]{1,0:T(8,128)}, f32[128,512]{1,0:T(8,128)S(1)}, u32[]{:S(2)}, u32[]{:S(2)}) %collective-permute-start.3) | collective-permute-done | bytes 262176 | tf_op jit(solution)/shard_map/ppermute | solution.py:193
  37.6 1.4 collective-permute-done.4.w3
  39.0 0.9 copy-done.1
  40.9 13.3 %all-to-all-start = ((f32[128,8,128]{2,1,0:T(8,128)}), f32[128,8,128]{2,1,0:T(8,128)S(1)}, u32[]{:S(2)}, u32[]{:S(2)}) async-start(f32[128,8,128]{2,1,0:T(8,128)} %bitcast.8), calls=%async_computation | async-start | bytes 1048576 | tf_op jit(solution)/shard_map/all_to_all | solution.py:247
  54.2 3.3 %collective-permute-start.11 = (f32[8,128,128]{2,1,0:T(8,128)S(1)}, f32[8,128,128]{2,1,0:T(8,128)}, u32[]{:S(2)}, u32[]{:S(2)}) collective-permute-start(f32[8,128,128]{2,1,0:T(8,128)S(1)} %join_kernel.1.refs_0_), channel_id=1, source_target_pairs={{0,192},{64,0},{128,64},{192,128},{1,193},{65,1},{129,65},{193,129... | collective-permute-start | bytes 1572872 | tf_op jit(solution)/shard_map/ppermute | solution.py:193
  57.5 1.0 slice.8
  58.6 14.7 %collective-permute-done.11.refs_2_ = f32[8,128,128]{2,1,0:T(8,128)} collective-permute-done((f32[8,128,128]{2,1,0:T(8,128)S(1)}, f32[8,128,128]{2,1,0:T(8,128)}, u32[]{:S(2)}, u32[]{:S(2)}) %collective-permute-start.11) | collective-permute-done | bytes 524320 | tf_op jit(solution)/shard_map/ppermute | solution.py:193
  73.3 1.0 slice.9
  74.2 3.7 %collective-permute-start.13 = (f32[4,128,128]{2,1,0:T(8,128)S(1)}, f32[4,128,128]{2,1,0:T(8,128)}, u32[]{:S(2)}, u32[]{:S(2)}) collective-permute-start(f32[4,128,128]{2,1,0:T(8,128)S(1)} %slice.9), channel_id=1, source_target_pairs={{0,192},{64,0},{128,64},{192,128},{1,193},{65,1},{129,65},{193,129... | collective-permute-start | bytes 786440 | tf_op jit(solution)/shard_map/ppermute | solution.py:193
  78.4 4.5 %collective-permute-done.13.refs_4_ = f32[4,128,128]{2,1,0:T(8,128)} collective-permute-done((f32[4,128,128]{2,1,0:T(8,128)S(1)}, f32[4,128,128]{2,1,0:T(8,128)}, u32[]{:S(2)}, u32[]{:S(2)}) %collective-permute-start.13) | collective-permute-done | bytes 262176 | tf_op jit(solution)/shard_map/ppermute | solution.py:193
  83.4 0.9 copy-done.4
  85.3 0.9 copy-done.8
  86.3 4.7 %beta_near_kernel.1 = (f32[16,128,128]{2,1,0:T(8,128)S(1)}, bf16[16,256,128]{2,1,0:T(8,128)(2,1)S(1)}) custom-call(s32[4]{0:T(128)S(1)} %pad_add_fusion.where, s32[128]{0:T(128)S(1)} %get-tuple-element.24.cols, s32[128]{0:T(128)S(1)} %get-tuple-element.23.slots, f32[128,512]{1,0:T(8,128)S(1)} %copy-done.2, f32[128,512]{1,0:T(8,128)S(1)} %copy-done.4, ...), custom_call_target="tpu_custom_call" | custom-call | flops 402653184 | bytes 7340032 | tf_op jit(solution)/shard_map/beta_near_kernel/pallas_call | solution.py:226
  91.0 1.0 copy-done.9
  92.0 1.0 copy-done.11
  93.0 5.3 %alpha_near_kernel.1 = (f32[32,32,128]{2,1,0:T(8,128)S(1)}, bf16[32,64,128]{2,1,0:T(8,128)(2,1)S(1)}) custom-call(s32[128]{0:T(128)S(1)} %get-tuple-element.24.cols, s32[128]{0:T(128)S(1)} %convert_reduce_fusion.owners, f32[32,32,128]{2,1,0:T(8,128)S(1)} %bitcast.12, f32[32,128,128]{2,1,0:T(8,128)S(1)} %copy-done, f32[32,128,128]{2,1,0:T(8,128)} %collective-permute-done.5.h1), custom_call_target="tpu_custom_call" | custom-call | flops 402653184 | bytes 7340032 | tf_op jit(solution)/shard_map/alpha_near_kernel/pallas_call | solution.py:226
  98.4 7.0 %far_kernel.1 = (f32[32,32,128]{2,1,0:T(8,128)}, f32[8,128,128]{2,1,0:T(8,128)S(1)}, f32[8,128,128]{2,1,0:T(8,128)S(1)}) custom-call(s32[4]{0:T(128)S(1)} %pad_add_fusion.where, s32[128]{0:T(128)S(1)} %get-tuple-element.24.cols, s32[128]{0:T(128)S(1)} %convert_reduce_fusion.owners, s32[128]{0:T(128)S(1)} %get-tuple-element.23.slots, ...), custom_call_target="tpu_custom_call" | custom-call | flops 402653184 | bytes 8388608 | tf_op jit(solution)/shard_map/far_kernel/pallas_call | solution.py:226
  105.4 16.2 %all-to-all-start.1 = ((f32[128,8,128]{2,1,0:T(8,128)}), f32[128,8,128]{2,1,0:T(8,128)S(1)}, u32[]{:S(2)}, u32[]{:S(2)}) async-start(f32[128,8,128]{2,1,0:T(8,128)} %bitcast.10), calls=%async_computation.1 | async-start | bytes 1048576 | tf_op jit(solution)/shard_map/all_to_all | solution.py:298
  121.8 1.9 %collective-permute-done.19.got_ref = f32[8,128,128]{2,1,0:T(8,128)S(1)} collective-permute-done((f32[8,128,128]{2,1,0:T(8,128)S(1)}, f32[8,128,128]{2,1,0:T(8,128)S(1)}, u32[]{:S(2)}, u32[]{:S(2)}) %collective-permute-start.19) | collective-permute-done | bytes 524320 | tf_op jit(solution)/shard_map/ppermute | solution.py:197
  123.7 3.4 %collective-permute-start.20 = (f32[4,128,128]{2,1,0:T(8,128)S(1)}, f32[4,128,128]{2,1,0:T(8,128)S(1)}, u32[]{:S(2)}, u32[]{:S(2)}) collective-permute-start(f32[4,128,128]{2,1,0:T(8,128)S(1)} %get-tuple-element.22), channel_id=1, source_target_pairs={{2,4},{4,2},{3,5},{5,3},{10,12},{12,10},{11,13},{13,11},{18,20},{2... | collective-permute-start | bytes 786440 | tf_op jit(solution)/shard_map/ppermute | solution.py:300
  127.1 11.8 %collective-permute-done.20.got_ref = f32[4,128,128]{2,1,0:T(8,128)S(1)} collective-permute-done((f32[4,128,128]{2,1,0:T(8,128)S(1)}, f32[4,128,128]{2,1,0:T(8,128)S(1)}, u32[]{:S(2)}, u32[]{:S(2)}) %collective-permute-start.20) | collective-permute-done | bytes 262176 | tf_op jit(solution)/shard_map/ppermute | solution.py:300
  139.0 2.3 %all-to-all-done.1 = f32[128,8,128]{2,1,0:T(8,128)S(1)} async-done(((f32[128,8,128]{2,1,0:T(8,128)}), f32[128,8,128]{2,1,0:T(8,128)S(1)}, u32[]{:S(2)}, u32[]{:S(2)}) %all-to-all-start.1) | async-done | bytes 524320 | tf_op jit(solution)/shard_map/all_to_all | solution.py:298
  (58 shorter events, 9.8 us)
Async XLA Ops:
  0.0 15.3 %collective-permute-start = (s32[32]{0:T(128)}, s32[32]{0:T(128)S(1)}, u32[]{:S(2)}, u32[]{:S(2)}) collective-permute-start(s32[32]{0:T(128)} %param.7), channel_id=1, source_target_pairs={{0,1},{1,0},{2,3},{3,2},{4,5},{5,4},{6,7},{7,6},{8,9},{9,8},{10,11... | collective-permute-start | bytes 392 | tf_op jit(solution)/shard_map/ppermute | solution.py:197
  0.0 82.9 %collective-permute-start.5 = (f32[32,128,128]{2,1,0:T(8,128)}, f32[32,128,128]{2,1,0:T(8,128)}, u32[]{:S(2)}, u32[]{:S(2)}) collective-permute-start(f32[32,128,128]{2,1,0:T(8,128)} %h0.3), channel_id=1, source_target_pairs={{0,1},{1,0},{2,3},{3,2},{4,5},{5,4},{6,7},{7,6},{8,9},{9,8},{10,11... | collective-permute-start | bytes 6291464 | tf_op jit(solution)/shard_map/ppermute | solution.py:197
  0.5 31.1 %collective-permute-start.2 = (f32[128,512]{1,0:T(8,128)}, f32[128,512]{1,0:T(8,128)S(1)}, u32[]{:S(2)}, u32[]{:S(2)}) collective-permute-start(f32[128,512]{1,0:T(8,128)} %w0.1), channel_id=1, source_target_pairs={{0,2},{2,4},{4,6},{6,0},{1,3},{3,5},{5,7},{7,1},{8,10},{10,12},{12... | collective-permute-start | bytes 786440 | tf_op jit(solution)/shard_map/ppermute | solution.py:193
  3.3 8.6 %collective-permute-start.6 = (f32[2,128,128]{2,1,0:T(8,128)S(1)}, f32[2,128,128]{2,1,0:T(8,128)S(1)}, u32[]{:S(2)}, u32[]{:S(2)}) collective-permute-start(f32[2,128,128]{2,1,0:T(8,128)S(1)} %constant_dynamic-slice_fusion), channel_id=1, source_target_pairs={{0,2},{2,0},{4,6},{6,4},{1,3},{3,1},{5,7},{7,5},{8,10},{10,8},{12,... | collective-permute-start | bytes 393224 | tf_op jit(solution)/shard_map/ppermute | solution.py:201
  12.0 10.6 %collective-permute-start.7 = (f32[2,128,128]{2,1,0:T(8,128)S(1)}, f32[2,128,128]{2,1,0:T(8,128)S(1)}, u32[]{:S(2)}, u32[]{:S(2)}) collective-permute-start(f32[2,128,128]{2,1,0:T(8,128)S(1)} %collective-permute-done.6.own), channel_id=1, source_target_pairs={{0,8},{8,16},{16,24},{24,0},{1,9},{9,17},{17,25},{25,1},{2,10},{10... | collective-permute-start | bytes 393224 | tf_op jit(solution)/shard_map/ppermute | solution.py:193
  13.5 10.1 %collective-permute-start.8 = (f32[2,128,128]{2,1,0:T(8,128)S(1)}, f32[2,128,128]{2,1,0:T(8,128)S(1)}, u32[]{:S(2)}, u32[]{:S(2)}) collective-permute-start(f32[2,128,128]{2,1,0:T(8,128)S(1)} %collective-permute-done.6.own), channel_id=1, source_target_pairs={{0,24},{8,0},{16,8},{24,16},{1,25},{9,1},{17,9},{25,17},{2,26},{10... | collective-permute-start | bytes 393224 | tf_op jit(solution)/shard_map/ppermute | solution.py:193
  16.0 4.0 %collective-permute-start.1 = (s32[64]{0:T(128)S(1)}, s32[64]{0:T(128)S(1)}, u32[]{:S(2)}, u32[]{:S(2)}) collective-permute-start(s32[64]{0:T(128)S(1)} %pad_add_fusion.1), channel_id=1, source_target_pairs={{0,2},{2,0},{4,6},{6,4},{1,3},{3,1},{5,7},{7,5},{8,10},{10,8},{12,... | collective-permute-start | bytes 776 | tf_op jit(solution)/shard_map/ppermute | solution.py:201
  20.0 17.6 %collective-permute-start.3 = (f32[128,512]{1,0:T(8,128)}, f32[128,512]{1,0:T(8,128)S(1)}, u32[]{:S(2)}, u32[]{:S(2)}) collective-permute-start(f32[128,512]{1,0:T(8,128)} %w0.1), channel_id=1, source_target_pairs={{0,4},{2,6},{4,0},{6,2},{1,5},{3,7},{5,1},{7,3},{8,12},{10,14},{12... | collective-permute-start | bytes 786440 | tf_op jit(solution)/shard_map/ppermute | solution.py:193
  22.6 16.4 %collective-permute-start.4 = (f32[128,512]{1,0:T(8,128)}, f32[128,512]{1,0:T(8,128)S(1)}, u32[]{:S(2)}, u32[]{:S(2)}) collective-permute-start(f32[128,512]{1,0:T(8,128)} %w0.1), channel_id=1, source_target_pairs={{0,6},{2,0},{4,2},{6,4},{1,7},{3,1},{5,3},{7,5},{8,14},{10,8},{12,... | collective-permute-start | bytes 786440 | tf_op jit(solution)/shard_map/ppermute | solution.py:193
  23.5 6.5 %collective-permute-start.9 = (f32[2,128,128]{2,1,0:T(8,128)S(1)}, f32[2,128,128]{2,1,0:T(8,128)S(1)}, u32[]{:S(2)}, u32[]{:S(2)}) collective-permute-start(f32[2,128,128]{2,1,0:T(8,128)S(1)} %collective-permute-done.6.own), channel_id=1, source_target_pairs={{0,16},{8,24},{16,0},{24,8},{1,17},{9,25},{17,1},{25,9},{2,18},{10... | collective-permute-start | bytes 393224 | tf_op jit(solution)/shard_map/ppermute | solution.py:193
  30.0 53.4 %copy-start.2 = (f32[128,512]{1,0:T(8,128)S(1)}, f32[128,512]{1,0:T(8,128)}, u32[]{:S(2)}) copy-start(f32[128,512]{1,0:T(8,128)} %w0.1) | copy-start | bytes 786436
  30.6 52.8 %copy-start = (f32[32,128,128]{2,1,0:T(8,128)S(1)}, f32[32,128,128]{2,1,0:T(8,128)}, u32[]{:S(2)}) copy-start(f32[32,128,128]{2,1,0:T(8,128)} %h0.3) | copy-start | bytes 6291460
  30.6 26.9 %collective-permute-start.10 = (f32[8,128,128]{2,1,0:T(8,128)S(1)}, f32[8,128,128]{2,1,0:T(8,128)}, u32[]{:S(2)}, u32[]{:S(2)}) collective-permute-start(f32[8,128,128]{2,1,0:T(8,128)S(1)} %join_kernel.1.refs_0_), channel_id=1, source_target_pairs={{0,64},{64,128},{128,192},{192,0},{1,65},{65,129},{129,193},{193,1... | collective-permute-start | bytes 1572872 | tf_op jit(solution)/shard_map/ppermute | solution.py:193
  31.6 9.3 %copy-start.3 = (f32[128,512]{1,0:T(8,128)}, f32[128,512]{1,0:T(8,128)S(1)}, u32[]{:S(2)}) copy-start(f32[128,512]{1,0:T(8,128)S(1)} %collective-permute-done.2.w1) | copy-start | bytes 786436
  37.6 3.3 %copy-start.5 = (f32[128,512]{1,0:T(8,128)}, f32[128,512]{1,0:T(8,128)S(1)}, u32[]{:S(2)}) copy-start(f32[128,512]{1,0:T(8,128)S(1)} %collective-permute-done.3.w2) | copy-start | bytes 786436
  40.9 52.1 %all-to-all-start = ((f32[128,8,128]{2,1,0:T(8,128)}), f32[128,8,128]{2,1,0:T(8,128)S(1)}, u32[]{:S(2)}, u32[]{:S(2)}) async-start(f32[128,8,128]{2,1,0:T(8,128)} %bitcast.8), calls=%async_computation | async-start | bytes 1048576 | tf_op jit(solution)/shard_map/all_to_all | solution.py:247
  54.2 19.1 %collective-permute-start.11 = (f32[8,128,128]{2,1,0:T(8,128)S(1)}, f32[8,128,128]{2,1,0:T(8,128)}, u32[]{:S(2)}, u32[]{:S(2)}) collective-permute-start(f32[8,128,128]{2,1,0:T(8,128)S(1)} %join_kernel.1.refs_0_), channel_id=1, source_target_pairs={{0,192},{64,0},{128,64},{192,128},{1,193},{65,1},{129,65},{193,129... | collective-permute-start | bytes 1572872 | tf_op jit(solution)/shard_map/ppermute | solution.py:193
  58.5 20.0 %collective-permute-start.12 = (f32[4,128,128]{2,1,0:T(8,128)S(1)}, f32[4,128,128]{2,1,0:T(8,128)}, u32[]{:S(2)}, u32[]{:S(2)}) collective-permute-start(f32[4,128,128]{2,1,0:T(8,128)S(1)} %slice.8), channel_id=1, source_target_pairs={{0,64},{64,128},{128,192},{192,0},{1,65},{65,129},{129,193},{193,1... | collective-permute-start | bytes 786440 | tf_op jit(solution)/shard_map/ppermute | solution.py:193
  74.2 8.7 %collective-permute-start.13 = (f32[4,128,128]{2,1,0:T(8,128)S(1)}, f32[4,128,128]{2,1,0:T(8,128)}, u32[]{:S(2)}, u32[]{:S(2)}) collective-permute-start(f32[4,128,128]{2,1,0:T(8,128)S(1)} %slice.9), channel_id=1, source_target_pairs={{0,192},{64,0},{128,64},{192,128},{1,193},{65,1},{129,65},{193,129... | collective-permute-start | bytes 786440 | tf_op jit(solution)/shard_map/ppermute | solution.py:193
  77.9 20.4 %collective-permute-start.14 = (f32[8,128,128]{2,1,0:T(8,128)S(1)}, f32[8,128,128]{2,1,0:T(8,128)}, u32[]{:S(2)}, u32[]{:S(2)}) collective-permute-start(f32[8,128,128]{2,1,0:T(8,128)S(1)} %join_kernel.1.refs_0_), channel_id=1, source_target_pairs={{0,1},{1,0},{2,3},{3,2},{4,5},{5,4},{6,7},{7,6},{8,9},{9,8},{10,11... | collective-permute-start | bytes 1572872 | tf_op jit(solution)/shard_map/ppermute | solution.py:197
  77.9 20.5 %collective-permute-start.15 = (f32[8,128,128]{2,1,0:T(8,128)}, f32[8,128,128]{2,1,0:T(8,128)}, u32[]{:S(2)}, u32[]{:S(2)}) collective-permute-start(f32[8,128,128]{2,1,0:T(8,128)} %collective-permute-done.10.refs_1_), channel_id=1, source_target_pairs={{0,1},{1,0},{2,3},{3,2},{4,5},{5,4},{6,7},{7,6},{8,9},{9,8},{10,11... | collective-permute-start | bytes 1572872 | tf_op jit(solution)/shard_map/ppermute | solution.py:197
  78.4 20.0 %collective-permute-start.16 = (f32[8,128,128]{2,1,0:T(8,128)}, f32[8,128,128]{2,1,0:T(8,128)}, u32[]{:S(2)}, u32[]{:S(2)}) collective-permute-start(f32[8,128,128]{2,1,0:T(8,128)} %collective-permute-done.11.refs_2_), channel_id=1, source_target_pairs={{0,1},{1,0},{2,3},{3,2},{4,5},{5,4},{6,7},{7,6},{8,9},{9,8},{10,11... | collective-permute-start | bytes 1572872 | tf_op jit(solution)/shard_map/ppermute | solution.py:197
  82.9 15.5 %collective-permute-start.17 = (f32[4,128,128]{2,1,0:T(8,128)}, f32[4,128,128]{2,1,0:T(8,128)}, u32[]{:S(2)}, u32[]{:S(2)}) collective-permute-start(f32[4,128,128]{2,1,0:T(8,128)} %collective-permute-done.12.refs_3_), channel_id=1, source_target_pairs={{0,1},{1,0},{2,3},{3,2},{4,5},{5,4},{6,7},{7,6},{8,9},{9,8},{10,11... | collective-permute-start | bytes 786440 | tf_op jit(solution)/shard_map/ppermute | solution.py:197
  82.9 15.5 %collective-permute-start.18 = (f32[4,128,128]{2,1,0:T(8,128)}, f32[4,128,128]{2,1,0:T(8,128)}, u32[]{:S(2)}, u32[]{:S(2)}) collective-permute-start(f32[4,128,128]{2,1,0:T(8,128)} %collective-permute-done.13.refs_4_), channel_id=1, source_target_pairs={{0,1},{1,0},{2,3},{3,2},{4,5},{5,4},{6,7},{7,6},{8,9},{9,8},{10,11... | collective-permute-start | bytes 786440 | tf_op jit(solution)/shard_map/ppermute | solution.py:197
  83.4 1.0 copy-start.4
  91.0 1.0 copy-start.9
  92.0 1.0 copy-start.11
  93.0 5.4 %copy-start.10 = (f32[16,128,128]{2,1,0:T(8,128)S(1)}, f32[16,128,128]{2,1,0:T(8,128)}, u32[]{:S(2)}) copy-start(f32[16,128,128]{2,1,0:T(8,128)} %copy-done.9) | copy-start | bytes 3145732
  93.0 5.4 %copy-start.12 = (bf16[16,256,128]{2,1,0:T(8,128)(2,1)S(1)}, bf16[16,256,128]{2,1,0:T(8,128)(2,1)}, u32[]{:S(2)}) copy-start(bf16[16,256,128]{2,1,0:T(8,128)(2,1)} %copy-done.11) | copy-start | bytes 3145732
  105.4 35.8 %all-to-all-start.1 = ((f32[128,8,128]{2,1,0:T(8,128)}), f32[128,8,128]{2,1,0:T(8,128)S(1)}, u32[]{:S(2)}, u32[]{:S(2)}) async-start(f32[128,8,128]{2,1,0:T(8,128)} %bitcast.10), calls=%async_computation.1 | async-start | bytes 1048576 | tf_op jit(solution)/shard_map/all_to_all | solution.py:298
  121.7 2.0 %collective-permute-start.19 = (f32[8,128,128]{2,1,0:T(8,128)S(1)}, f32[8,128,128]{2,1,0:T(8,128)S(1)}, u32[]{:S(2)}, u32[]{:S(2)}) collective-permute-start(f32[8,128,128]{2,1,0:T(8,128)S(1)} %get-tuple-element.20), channel_id=1, source_target_pairs={{0,1},{1,0},{2,3},{3,2},{4,5},{5,4},{6,7},{7,6},{8,9},{9,8},{10,11... | collective-permute-start | bytes 1572872 | tf_op jit(solution)/shard_map/ppermute | solution.py:197
  123.7 15.2 %collective-permute-start.20 = (f32[4,128,128]{2,1,0:T(8,128)S(1)}, f32[4,128,128]{2,1,0:T(8,128)S(1)}, u32[]{:S(2)}, u32[]{:S(2)}) collective-permute-start(f32[4,128,128]{2,1,0:T(8,128)S(1)} %get-tuple-element.22), channel_id=1, source_target_pairs={{2,4},{4,2},{3,5},{5,3},{10,12},{12,10},{11,13},{13,11},{18,20},{2... | collective-permute-start | bytes 786440 | tf_op jit(solution)/shard_map/ppermute | solution.py:300
  (4 other events, 3.8 us)
